TPU v7x, 32 devices: a whole 2x2x4 slice. The times are simulated.
32 devices in a mesh: seq: 8 (over z, x), exp: 4 (over y, core).
Axes of the slice: x: 2, y: 2, z: 4, core: 2. Of those that a mesh axis runs over, the one named last changes fastest.
Arguments:
- block_input: float32 [4096, 768], P(('seq', 'exp')), may hold values from -6 to 6
- seq_lengths: int32 [10], replicated, may hold values from 1 to 2048, 4096 in all
- expert_ids: int32 [4096, 1], P(('seq', 'exp')), may hold values from 0 to 3
- output_grad: float32 [4096, 768], P(('seq', 'exp')), may hold values from -6 to 6
- mixer_gain: float32 [768], replicated, may hold values from 0.5 to 1.5
- in_proj: float32 [768, 3072], replicated, may hold values from -0.21875 to 0.21875
- conv_weight: float32 [4, 1536], replicated, may hold values from -3 to 3
- conv_bias: float32 [1536], replicated, may hold values from -1.75 to 1.75
- state_proj: float32 [1536, 80], replicated, may hold values from -0.15625 to 0.15625
- step_proj: float32 [48, 1536], replicated, may hold values from -0.875 to 0.875
- step_bias: float32 [1536], replicated, may hold values from -7 to -2.5
- decay_log: float32 [1536, 16], replicated, may hold values from 0 to 2.77
- skip_gain: float32 [1536], replicated, may hold values from 0.5 to 1.5
- out_proj: float32 [1536, 768], replicated, may hold values from -0.3125 to 0.3125
- router_gain: float32 [768], replicated, may hold values from 0.5 to 1.5
- router: float32 [768, 4], replicated, may hold values from -0.15625 to 0.15625
- expert_up: float32 [4, 768, 3072], P('exp', None, 'seq'), may hold values from -0.21875 to 0.21875
- expert_down: float32 [4, 3072, 768], P('exp', 'seq'), may hold values from -0.875 to 0.875
Outputs:
- block_output: float32 [4096, 768], P(('seq', 'exp'))
- input_grad: float32 [4096, 768], P(('seq', 'exp'))
- grad_mixer_gain: float32 [768], replicated
- grad_in_proj: float32 [768, 3072], replicated
- grad_conv_weight: float32 [4, 1536], replicated
- grad_conv_bias: float32 [1536], replicated
- grad_state_proj: float32 [1536, 80], replicated
- grad_step_proj: float32 [48, 1536], replicated
- grad_step_bias: float32 [1536], replicated
- grad_decay_log: float32 [1536, 16], replicated
- grad_skip_gain: float32 [1536], replicated
- grad_out_proj: float32 [1536, 768], replicated
- grad_router_gain: float32 [768], replicated
- grad_router: float32 [768, 4], replicated
- grad_expert_up: float32 [4, 768, 3072], P('exp', None, 'seq')
- grad_expert_down: float32 [4, 3072, 768], P('exp', 'seq')
- expert_load: int32 [4], replicated
- dropped_load: int32 [4], replicated
All inputs are finite; a program needn't handle non-finite values.
Results may differ from a plain program's by a relative error of at most 0.0003.
Values sent between devices are 32-bit elements; how exact they have to be, the bound alone decides.
No kernel may reach another device: no remote copies, remote signals or barrier semaphores. Data moves between devices by JAX's collectives and lax.ppermute only.
A program may use at most 448 MiB of HBM per device.

v0:
```python
import jax
import jax.numpy as jnp
from jax import lax
from jax.sharding import PartitionSpec as P

precise = lax.Precision.HIGHEST
epsilon = 1e-05


def passed_along(block, axis, distance):
    devices = range(lax.axis_size(axis))
    route = [(i - distance, i) for i in devices if i - distance in devices]
    return lax.ppermute(block, axis, route)


def entering(value, axis, join, neutral, backward):
    count, mine = (lax.axis_size(axis), lax.axis_index(axis))
    pieces = jax.tree.map(lambda part: lax.all_gather(part, axis), value)
    if backward:
        pieces = jax.tree.map(lambda part: part[::-1], pieces)
        mine = count - 1 - mine
    so_far = jax.tree.map(
        lambda part, zero: jnp.full_like(part, 0) + jnp.asarray(zero, part.dtype), value, neutral
    )

    def lap(position, so_far):
        longer = join(so_far, jax.tree.map(lambda part: part[position], pieces))
        return jax.tree.map(lambda new, old: jnp.where(position < mine, new, old), longer, so_far)

    return lax.fori_loop(0, count - 1, lap, so_far)


def matmul_high(left, right):
    return jnp.dot(left, right, precision=precise, preferred_element_type=jnp.float32)


def rms_scale(values_in, gain):
    return (
        values_in
        * lax.rsqrt(jnp.mean(values_in * values_in, axis=1, keepdims=True) + epsilon)
        * gain
    )


def chain_states(earlier, later):
    return (later[0] * earlier[0], later[0] * earlier[1] + later[1])


def per_device(
    block_input,
    seq_lengths,
    expert_ids,
    output_grad,
    mixer_gain,
    in_proj,
    conv_weight,
    conv_bias,
    state_proj,
    step_proj,
    step_bias,
    decay_log,
    skip_gain,
    out_proj,
    router_gain,
    router,
    expert_up,
    expert_down,
):
    tokens_n = block_input.shape[0]
    kernel_taps = conv_weight.shape[0]
    inner_width = in_proj.shape[1] // 2
    low_rank = step_proj.shape[0]
    state_size = decay_log.shape[1]
    experts_n = router.shape[1]
    capacity = (5 * tokens_n + 4 * experts_n - 1) // (4 * experts_n)
    span_index = lax.axis_index(("seq", "exp"))
    span_first = span_index * tokens_n
    position = span_first + jnp.arange(tokens_n, dtype=jnp.int32)
    seq_starts = jnp.cumsum(seq_lengths) - seq_lengths
    before = seq_starts[None, :] <= position[:, None]
    own_start = jnp.max(jnp.where(before, seq_starts[None, :], 0), axis=1)
    fresh = (own_start == position).astype(jnp.float32)
    alive = (own_start < span_first).astype(jnp.float32)
    tap_pos = (
        position[:, None] - (kernel_taps - 1) + jnp.arange(kernel_taps, dtype=jnp.int32)[None, :]
    )
    tap_valid = (tap_pos >= own_start[:, None]).astype(jnp.float32)

    def project_in(block_input, mixer_gain, in_proj):
        joined = matmul_high(rms_scale(block_input, mixer_gain), in_proj)
        return (joined[:, :inner_width], joined[:, inner_width:])

    def conv_features(extended, conv_weight, conv_bias, state_proj, step_proj, step_bias):
        summed = jnp.broadcast_to(conv_bias[None, :], (tokens_n, inner_width))
        for offset in range(kernel_taps):
            summed = (
                summed
                + extended[offset : offset + tokens_n]
                * tap_valid[:, offset : offset + 1]
                * conv_weight[offset][None, :]
            )
        activated = jax.nn.silu(summed)
        projected = matmul_high(activated, state_proj)
        step_sizes = jax.nn.softplus(matmul_high(projected[:, :low_rank], step_proj) + step_bias)
        return (
            activated,
            step_sizes,
            projected[:, low_rank : low_rank + state_size],
            projected[:, low_rank + state_size :],
        )

    def scan_part(activated, step_sizes, in_state, out_state, decay_log):
        decay_rate = -jnp.exp(decay_log)
        block_len = min(32, tokens_n)
        blocks = tokens_n // block_len

        def advance(carried, pieces):
            act_b, step_b, in_b, out_b, fresh_b = pieces
            outputs = []
            for index in range(block_len):
                decay_now = jnp.exp(step_b[index][:, None] * decay_rate) * (1.0 - fresh_b[index])
                carried = (
                    decay_now * carried
                    + (step_b[index] * act_b[index])[:, None] * in_b[index][None, :]
                )
                outputs.append(jnp.sum(carried * out_b[index][None, :], axis=1))
            return (carried, jnp.stack(outputs))

        pieces = tuple(
            (
                member.reshape((blocks, block_len) + member.shape[1:])
                for member in (activated, step_sizes, in_state, out_state, fresh)
            )
        )
        zero_end, local_out = lax.scan(advance, jnp.zeros(decay_log.shape, jnp.float32), pieces)
        running_end = jnp.sum(step_sizes, axis=0)
        end_decay = jnp.exp(running_end[:, None] * decay_rate) * alive[tokens_n - 1]
        return (local_out.reshape(tokens_n, -1), zero_end, end_decay)

    def carry_terms(out_state, step_sizes, decay_log, start_state):
        decay_rate = -jnp.exp(decay_log)
        running = jnp.cumsum(step_sizes, axis=0)
        block_len = min(64, tokens_n)
        blocks = tokens_n // block_len

        def one_block(pieces):
            run_b, out_b, alive_b = pieces
            factor = jnp.exp(run_b[:, :, None] * decay_rate[None]) * start_state[None]
            return jnp.sum(factor * out_b[:, None, :], axis=2) * alive_b[:, None]

        shaped = (
            running.reshape(blocks, block_len, -1),
            out_state.reshape(blocks, block_len, -1),
            alive.reshape(blocks, block_len),
        )
        return lax.map(one_block, shaped).reshape(tokens_n, -1)

    def mixer_out(scan_out, activated, gate_z, skip_gain, out_proj, block_input):
        return block_input + matmul_high(
            (scan_out + skip_gain * activated) * jax.nn.silu(gate_z), out_proj
        )

    chosen = (expert_ids == jnp.arange(experts_n, dtype=jnp.int32)[None, :]).astype(jnp.float32)

    def route(resid, router_gain, router):
        normed_moe = rms_scale(resid, router_gain)
        probs = jax.nn.softmax(matmul_high(normed_moe, router), axis=1)
        return (normed_moe, jnp.sum(probs * chosen, axis=1))

    (inner_x, gate_z), proj_back = jax.vjp(project_in, block_input, mixer_gain, in_proj)
    previous = passed_along(inner_x[tokens_n - kernel_taps + 1 :], ("seq", "exp"), 1)
    extended = jnp.concatenate([previous, inner_x], axis=0)
    (activated, step_sizes, in_state, out_state), conv_back = jax.vjp(
        conv_features, extended, conv_weight, conv_bias, state_proj, step_proj, step_bias
    )
    (local_out, zero_end, end_decay), scan_back = jax.vjp(
        scan_part, activated, step_sizes, in_state, out_state, decay_log
    )
    identity_pair = (jnp.ones_like(end_decay), jnp.zeros_like(zero_end))
    start_state = entering(
        (end_decay, zero_end), ("seq", "exp"), chain_states, identity_pair, False
    )[1]
    correction, carry_back = jax.vjp(carry_terms, out_state, step_sizes, decay_log, start_state)
    scan_out = local_out + correction
    resid, mixer_back = jax.vjp(
        mixer_out, scan_out, activated, gate_z, skip_gain, out_proj, block_input
    )
    (normed_moe, gate), route_back = jax.vjp(route, resid, router_gain, router)
    ahead_count = jnp.cumsum(chosen, axis=0) - chosen
    slot_rank = jnp.sum(ahead_count * chosen, axis=1).astype(jnp.int32)
    kept = (slot_rank < capacity).astype(jnp.float32)
    slot_ids = expert_ids[:, 0] * capacity + slot_rank
    dispatch = (
        jnp.arange(experts_n * capacity, dtype=jnp.int32)[:, None] == slot_ids[None, :]
    ).astype(jnp.float32) * kept[None, :]
    buffer = matmul_high(dispatch, normed_moe).reshape(experts_n, capacity, -1)
    full_up, full_down = (
        lax.all_gather(expert_up, "seq", axis=2, tiled=True),
        lax.all_gather(expert_down, "seq", axis=1, tiled=True),
    )
    received = lax.all_to_all(buffer, "exp", split_axis=0, concat_axis=0, tiled=True)
    local_n = full_up.shape[0]
    items = received.shape[1]
    grouped = received.reshape(-1, local_n, items, received.shape[2])
    hidden_pre = jnp.einsum("secd,edf->secf", grouped, full_up, precision=precise)
    result = jnp.einsum("secf,efd->secd", jax.nn.gelu(hidden_pre), full_down, precision=precise)
    returned = lax.all_to_all(
        result.reshape(received.shape), "exp", split_axis=0, concat_axis=0, tiled=True
    )
    returned, received, hidden_pre = (
        returned,
        received,
        hidden_pre.reshape(received.shape[0], items, -1),
    )
    combined = jnp.einsum(
        "st,sd->td", dispatch, returned.reshape(experts_n * capacity, -1), precision=precise
    )
    block_output = resid + gate[:, None] * combined
    grad_gate = jnp.sum(output_grad * combined, axis=1)
    grad_back = jnp.einsum(
        "st,td->sd", dispatch, output_grad * gate[:, None], precision=precise
    ).reshape(experts_n, capacity, -1)
    grad_result = lax.all_to_all(grad_back, "exp", split_axis=0, concat_axis=0, tiled=True)
    use_up, use_down = (
        lax.all_gather(expert_up, "seq", axis=2, tiled=True),
        lax.all_gather(expert_down, "seq", axis=1, tiled=True),
    )
    local_n = use_up.shape[0]
    sources = grad_result.shape[0] // local_n
    grad_group = grad_result.reshape(sources, local_n, capacity, -1)
    hidden_group = hidden_pre.reshape(sources, local_n, capacity, -1)
    input_group = received.reshape(sources, local_n, capacity, -1)
    gelu_hidden, gelu_back = jax.vjp(jax.nn.gelu, hidden_group)
    grad_down_full = jnp.einsum("secf,secd->efd", gelu_hidden, grad_group, precision=precise)
    grad_hidden = gelu_back(jnp.einsum("secd,efd->secf", grad_group, use_down, precision=precise))[
        0
    ]
    grad_up_full = jnp.einsum("secd,secf->edf", input_group, grad_hidden, precision=precise)
    grad_received = jnp.einsum("secf,edf->secd", grad_hidden, use_up, precision=precise).reshape(
        grad_result.shape
    )
    grad_buffer = lax.all_to_all(grad_received, "exp", split_axis=0, concat_axis=0, tiled=True)
    grad_expert_up, grad_expert_down = (
        lax.psum_scatter(grad_up_full, "seq", scatter_dimension=2, tiled=True),
        lax.psum_scatter(grad_down_full, "seq", scatter_dimension=1, tiled=True),
    )
    grad_normed_moe = jnp.einsum(
        "st,sd->td", dispatch, grad_buffer.reshape(experts_n * capacity, -1), precision=precise
    )
    grad_resid_route, grad_router_gain, grad_router = route_back((grad_normed_moe, grad_gate))
    grad_resid = output_grad + grad_resid_route
    grad_scan, grad_act_mix, grad_gate_z, grad_skip_gain, grad_out_proj, grad_input_mix = (
        mixer_back(grad_resid)
    )
    grad_out_carry, grad_step_carry, grad_decay_carry, grad_start = carry_back(grad_scan)
    grad_end = entering((end_decay, grad_start), ("seq", "exp"), chain_states, identity_pair, True)[
        1
    ]
    grad_act_scan, grad_step_scan, grad_in_state, grad_out_scan, grad_decay_scan = scan_back(
        (grad_scan, grad_end, grad_end * start_state)
    )
    (
        grad_extended,
        grad_conv_weight,
        grad_conv_bias,
        grad_state_proj,
        grad_step_proj,
        grad_step_bias,
    ) = conv_back(
        (
            grad_act_mix + grad_act_scan,
            grad_step_carry + grad_step_scan,
            grad_in_state,
            grad_out_carry + grad_out_scan,
        )
    )
    edge_grad = passed_along(grad_extended[: kernel_taps - 1], ("seq", "exp"), -1)
    grad_inner = grad_extended[kernel_taps - 1 :] + jnp.concatenate(
        [jnp.zeros((tokens_n - kernel_taps + 1, inner_width), jnp.float32), edge_grad], axis=0
    )
    grad_input_proj, grad_mixer_gain, grad_in_proj = proj_back((grad_inner, grad_gate_z))
    input_grad = grad_input_mix + grad_input_proj
    grad_decay_log = grad_decay_carry + grad_decay_scan
    load_local = jnp.sum(chosen, axis=0)
    drop_local = jnp.sum(chosen * (1.0 - kept)[:, None], axis=0)
    summed_grads = lax.psum(
        (
            grad_mixer_gain,
            grad_in_proj,
            grad_conv_weight,
            grad_conv_bias,
            grad_state_proj,
            grad_step_proj,
            grad_step_bias,
            grad_decay_log,
            grad_skip_gain,
            grad_out_proj,
            grad_router_gain,
            grad_router,
            load_local,
            drop_local,
        ),
        ("seq", "exp"),
    )
    expert_load = summed_grads[12].astype(jnp.int32)
    dropped_load = summed_grads[13].astype(jnp.int32)
    return (
        block_output,
        input_grad,
        summed_grads[0],
        summed_grads[1],
        summed_grads[2],
        summed_grads[3],
        summed_grads[4],
        summed_grads[5],
        summed_grads[6],
        summed_grads[7],
        summed_grads[8],
        summed_grads[9],
        summed_grads[10],
        summed_grads[11],
        grad_expert_up,
        grad_expert_down,
        expert_load,
        dropped_load,
    )


def solution(mesh):
    in_specs = (
        P(("seq", "exp"), None),
        P(),
        P(("seq", "exp"), None),
        P(("seq", "exp"), None),
        P(),
        P(),
        P(),
        P(),
        P(),
        P(),
        P(),
        P(),
        P(),
        P(),
        P(),
        P(),
        P("exp", None, "seq"),
        P("exp", "seq", None),
    )
    out_specs = (
        P(("seq", "exp"), None),
        P(("seq", "exp"), None),
        P(),
        P(),
        P(),
        P(),
        P(),
        P(),
        P(),
        P(),
        P(),
        P(),
        P(),
        P(),
        P("exp", None, "seq"),
        P("exp", "seq", None),
        P(),
        P(),
    )
    return jax.shard_map(
        per_device, mesh=mesh, in_specs=in_specs, out_specs=out_specs, check_vma=False
    )
```

profile of v0, /device:TPU:0, one launch (start us, length us, event | category | flops | bytes accessed | tf_op | source)
XLA Modules:
  0.0 3072.7 jit_solution(16956716026353753182)
XLA Ops:
  9.0 7.8 fusion.626
  16.8 2.5 collective-permute-start
  26.3 3.7 fusion.620
  31.8 3.1 fusion.703
  36.6 739.4 %while.750 = (s32[]{:T(128)}, f32[1536,16]{0,1:T(8,128)S(1)}, f32[4,32,1536]{2,1,0:T(8,128)}, f32[4,1536,1]{1,2,0:T(1,128)}, f32[4,1536,16]{1,2,0:T(8,128)}, /*i...) while((s32[]{:T(128)}, f32[1536,16]{0,1:T(8,128)S(1)}, ...), condition=%wide.region_36.37_spmd.clone, body=%wide.region_3.36_spmd.clone.sunk | while | flops 11132994 | bytes 24794744 | solution.py:135
  81.2 2.8 bitcast_dynamic-update-slice_fusion.107
  265.8 2.8 bitcast_dynamic-update-slice_fusion.107
  450.5 2.8 bitcast_dynamic-update-slice_fusion.107
  635.2 2.8 bitcast_dynamic-update-slice_fusion.107
  785.7 52.7 %all-gather.15.cloned.1.call-done = f32[49152,16]{0,1:T(8,128)} async-done(((f32[1536,16]{0,1:T(8,128)}), f32[49152,16]{0,1:T(8,128)}) %all-gather.15.cloned.1.call-update) | async-done | bytes 3145744 | tf_op jit(solution)/shard_map/all_gather | solution.py:18
  838.5 5.4 copy.107
  843.9 56.0 %all-gather.13.cloned.1.call-done = f32[49152,16]{0,1:T(8,128)} async-done(((f32[1536,16]{0,1:T(8,128)}), f32[49152,16]{0,1:T(8,128)}) %all-gather.13.cloned.1.call-update) | async-done | bytes 3145744 | tf_op jit(solution)/shard_map/all_gather | solution.py:18
  899.8 3.8 copy.120
  903.7 68.8 %while.751 = (s32[]{:T(128)}, f32[1536,16]{0,1:T(8,128)S(1)}, s32[]{:T(128)}, f32[32,1536,16]{1,2,0:T(8,128)}, f32[32,1536,16]{1,0,2:T(8,128)}, /*index=5*/s32[]{:T(128)}, s32[]{:T(128)}) while((s32[]{:T(128)}, f32[1536,16]{0,1:T(8,128)S(1)}, s32[]{:T(128)}, f32[32,1536,16]{1,2,0:T(8,128)}, f32[32,1536,16]{1,0,2:T(8,128)}, ...), condition=%wide.region_40.41_spmd.clone, body=%wide.region_39.40_spmd.clone.sunk | while | flops 98308 | bytes 589929 | solution.py:30
  973.4 25.3 while.749
  978.1 6.1 multiply_dynamic-update-slice_fusion.38
  990.7 6.3 multiply_dynamic-update-slice_fusion.38
  1000.8 5.6 multiply_reduce_fusion.141
  1008.6 3.7 all-to-all-start
  1012.8 7.9 all-to-all-done
  1021.5 17.0 all-gather.9.cloned.1.call-done
  1038.5 8.4 fusion.586
  1046.9 129.9 %all-gather.11.cloned.1.call-done = f32[1,3072,768]{2,1,0:T(8,128)} async-done(((f32[1,384,768]{2,1,0:T(8,128)}), f32[1,3072,768]{2,1,0:T(8,128)}) %all-gather.11.cloned.1.call-update) | async-done | bytes 9437200 | tf_op jit(solution)/shard_map/all_gather | solution.py:199
  1176.8 9.3 fusion.580
  1186.1 4.1 all-to-all-start.1
  1192.9 5.9 all-to-all-done.1
  1204.4 11.1 all_to_all.20
  1215.5 13.0 fusion.598
  1229.9 13.1 fusion.582
  1243.0 3.6 all-to-all-start.3
  1247.7 7.3 all-to-all-done.3
  1258.2 9.3 multiply_reduce_fusion.131
  1269.1 23.9 while.752
  1271.6 7.2 multiply_reduce_fusion.199
  1283.5 7.2 multiply_reduce_fusion.199
  1293.9 4.0 rev.6
  1299.4 15.4 reduce_window_sum.42
  1314.8 7.2 fusion.700
  1322.1 28.1 all-gather.17.cloned.1.call-done
  1350.2 5.4 copy.108
  1355.6 8.1 rev.7
  1363.7 68.2 %while.753 = (s32[]{:T(128)}, f32[1536,16]{0,1:T(8,128)S(1)}, s32[]{:T(128)}, f32[32,1536,16]{1,2,0:T(8,128)}, f32[32,1536,16]{1,0,2:T(8,128)}, /*index=5*/s32[]{:T(128)}, s32[]{:T(128)}) while((s32[]{:T(128)}, f32[1536,16]{0,1:T(8,128)S(1)}, s32[]{:T(128)}, f32[32,1536,16]{1,2,0:T(8,128)}, f32[32,1536,16]{1,0,2:T(8,128)}, ...), condition=%wide.region_60.61_spmd.clone, body=%wide.region_59.60_spmd.clone.sunk | while | flops 98308 | bytes 589929 | solution.py:30
  1435.2 710.6 %while.754 = (s32[]{:T(128)}, f32[1536,16]{0,1:T(8,128)}, f32[1536,16]{0,1:T(8,128)S(1)}, f32[4,32,1536]{2,1,0:T(8,128)}, f32[4,32,1536]{2,1,0:T(8,128)}, /*inde...) while((s32[]{:T(128)}, f32[1536,16]{0,1:T(8,128)}, ...), condition=%wide.region_190.191_spmd.clone, body=%wide.region_61.190_spmd.clone.sunk | while | flops 17356836 | bytes 57770112 | solution.py:135
  1464.6 13.3 multiply_reduce_fusion.200
  1507.0 15.2 multiply_reduce_fusion.201
  1610.6 2.8 multiply_add_fusion.56
  1642.2 13.3 multiply_reduce_fusion.200
  1684.4 15.2 multiply_reduce_fusion.201
  1788.0 2.8 multiply_add_fusion.56
  1819.7 13.3 multiply_reduce_fusion.200
  1862.1 15.2 multiply_reduce_fusion.201
  1965.2 2.8 multiply_add_fusion.56
  1996.8 13.3 multiply_reduce_fusion.200
  2039.2 15.2 multiply_reduce_fusion.201
  2142.8 2.8 multiply_add_fusion.56
  2160.5 10.1 fusion.603
  2172.2 10.4 convolution_bitcast_fusion
  2184.4 10.3 convolution_bitcast_fusion.1
  2196.3 12.1 multiply_reduce_fusion.137
  2208.5 44.7 %all-reduce.174 = (f32[768]{0:T(1024)}, f32[4,1536]{1,0:T(4,128)}, f32[1536]{0:T(1024)}, f32[1536]{0:T(1024)}, f32[1536]{0:T(1024)}, /*index=5*/f32[768]{0:T(102...) all-reduce(f32[768]{0:T(1024)S(1)} %get-tuple-element.12840, ...), channel_id=1, replica_groups=mesh['seq'=8,'exp'=4] {'seq','exp'}, use_global_device_ids=true, to_apply=%region_195.196 | all-reduce | flops 15368 | bytes 122944 | tf_op jit(solution)/shard_map/psum | solution.py:286
  2255.1 459.9 %all-reduce.178.cloned.1.call-done = (f32[768,3072]{1,0:T(8,128)}, f32[1536,80]{0,1:T(8,128)}, f32[48,1536]{1,0:T(8,128)}, f32[1536,16]{0,1:T(8,128)}, f32[1536,768]{1,0:T(8,128)}) async-done(((f32[768,3072]{1,0:T(8,128)}, f32[1536,80]{0,1:T(8,128)}, f32[48,1536]{1,0:T(8,128)}, f32[1536,16]{0,1:T(8,128)}, f32[1536,768]{1,0:T(8,128)}), (f32[768,3072]{1,0:T(8,128)}, f32[1536,80]{0,1:T(8,128)}, ...) | async-done | bytes 15040528 | tf_op jit(solution)/shard_map/psum | solution.py:286
  2715.1 170.9 %reduce-scatter.5.cloned.1.call-done = f32[1,384,768]{2,1,0:T(8,128)} async-done(((f32[1,3072,768]{2,1,0:T(8,128)}), f32[1,384,768]{2,1,0:T(8,128)}) %reduce-scatter.5.cloned.1.call-update) | async-done | bytes 1179664 | tf_op jit(solution)/shard_map/reduce_scatter | solution.py:245
  2885.9 166.6 %reduce-scatter.3.cloned.1.call-done = f32[1,768,384]{2,1,0:T(8,128)} async-done(((f32[1,768,3072]{2,1,0:T(8,128)}), f32[1,768,384]{2,1,0:T(8,128)}) %reduce-scatter.3.cloned.1.call-update) | async-done | bytes 1179664 | tf_op jit(solution)/shard_map/reduce_scatter | solution.py:244
  3052.5 8.8 copy.1512
  (3602 shorter events, 1452.1 us)
Async XLA Ops:
  7.2 831.3 %all-gather.15.cloned.1.call-start = ((), (), s32[]{:S(2)}) async-start(), calls=%async_computation.11 | async-start | bytes 3244032 | tf_op jit(solution)/shard_map/all_gather | solution.py:18
  16.8 9.4 collective-permute-start
  113.4 108.3 %copy-start.100 = (f32[4,32,16]{2,1,0:T(8,128)S(1)}, f32[4,32,16]{2,1,0:T(8,128)}, u32[]{:S(2)}) copy-start(f32[4,32,16]{2,1,0:T(8,128)} %copy-done.99) | copy-start | bytes 24580 | tf_op jit(solution)/shard_map/jvp()/while
  113.4 108.3 %copy-start.192 = (f32[4,1,16]{2,1,0:T(1,128)S(1)}, f32[4,1,16]{2,1,0:T(1,128)}, u32[]{:S(2)}) copy-start(f32[4,1,16]{2,1,0:T(1,128)} %copy-done.191) | copy-start | bytes 772 | tf_op jit(solution)/shard_map/jvp()/while
  117.0 104.5 %copy-start.205 = (f32[4]{0:T(128)}, f32[4]{0:T(128)S(1)}, u32[]{:S(2)}) copy-start(f32[4]{0:T(128)S(1)} %get-tuple-element.21621) | copy-start | bytes 52 | tf_op jit(solution)/shard_map/jvp()/while
  117.0 104.5 %copy-start.221 = (f32[4]{0:T(128)}, f32[4]{0:T(128)S(1)}, u32[]{:S(2)}) copy-start(f32[4]{0:T(128)S(1)} %get-tuple-element.21632) | copy-start | bytes 52 | tf_op jit(solution)/shard_map/jvp()/while
  117.1 104.4 %copy-start.225 = (f32[4]{0:T(128)}, f32[4]{0:T(128)S(1)}, u32[]{:S(2)}) copy-start(f32[4]{0:T(128)S(1)} %get-tuple-element.21642) | copy-start | bytes 52 | tf_op jit(solution)/shard_map/jvp()/while
  117.1 104.4 %copy-start.227 = (f32[4]{0:T(128)}, f32[4]{0:T(128)S(1)}, u32[]{:S(2)}) copy-start(f32[4]{0:T(128)S(1)} %get-tuple-element.21652) | copy-start | bytes 52 | tf_op jit(solution)/shard_map/jvp()/while
  117.2 104.4 %copy-start.229 = (f32[4]{0:T(128)}, f32[4]{0:T(128)S(1)}, u32[]{:S(2)}) copy-start(f32[4]{0:T(128)S(1)} %get-tuple-element.21662) | copy-start | bytes 52 | tf_op jit(solution)/shard_map/jvp()/while
  117.2 104.4 %copy-start.231 = (f32[4]{0:T(128)}, f32[4]{0:T(128)S(1)}, u32[]{:S(2)}) copy-start(f32[4]{0:T(128)S(1)} %get-tuple-element.21672) | copy-start | bytes 52 | tf_op jit(solution)/shard_map/jvp()/while
  117.3 104.3 %copy-start.233 = (f32[4]{0:T(128)}, f32[4]{0:T(128)S(1)}, u32[]{:S(2)}) copy-start(f32[4]{0:T(128)S(1)} %get-tuple-element.21682) | copy-start | bytes 52 | tf_op jit(solution)/shard_map/jvp()/while
  117.3 104.3 %copy-start.235 = (f32[4]{0:T(128)}, f32[4]{0:T(128)S(1)}, u32[]{:S(2)}) copy-start(f32[4]{0:T(128)S(1)} %get-tuple-element.21692) | copy-start | bytes 52 | tf_op jit(solution)/shard_map/jvp()/while
  117.4 104.2 %copy-start.196 = (f32[4]{0:T(128)}, f32[4]{0:T(128)S(1)}, u32[]{:S(2)}) copy-start(f32[4]{0:T(128)S(1)} %get-tuple-element.21712) | copy-start | bytes 52 | tf_op jit(solution)/shard_map/jvp()/while
  117.4 104.2 %copy-start.237 = (f32[4]{0:T(128)}, f32[4]{0:T(128)S(1)}, u32[]{:S(2)}) copy-start(f32[4]{0:T(128)S(1)} %get-tuple-element.21702) | copy-start | bytes 52 | tf_op jit(solution)/shard_map/jvp()/while
  298.1 108.3 %copy-start.100 = (f32[4,32,16]{2,1,0:T(8,128)S(1)}, f32[4,32,16]{2,1,0:T(8,128)}, u32[]{:S(2)}) copy-start(f32[4,32,16]{2,1,0:T(8,128)} %copy-done.99) | copy-start | bytes 24580 | tf_op jit(solution)/shard_map/jvp()/while
  298.1 108.3 %copy-start.192 = (f32[4,1,16]{2,1,0:T(1,128)S(1)}, f32[4,1,16]{2,1,0:T(1,128)}, u32[]{:S(2)}) copy-start(f32[4,1,16]{2,1,0:T(1,128)} %copy-done.191) | copy-start | bytes 772 | tf_op jit(solution)/shard_map/jvp()/while
  301.7 104.5 %copy-start.205 = (f32[4]{0:T(128)}, f32[4]{0:T(128)S(1)}, u32[]{:S(2)}) copy-start(f32[4]{0:T(128)S(1)} %get-tuple-element.21621) | copy-start | bytes 52 | tf_op jit(solution)/shard_map/jvp()/while
  301.7 104.5 %copy-start.221 = (f32[4]{0:T(128)}, f32[4]{0:T(128)S(1)}, u32[]{:S(2)}) copy-start(f32[4]{0:T(128)S(1)} %get-tuple-element.21632) | copy-start | bytes 52 | tf_op jit(solution)/shard_map/jvp()/while
  301.8 104.4 %copy-start.225 = (f32[4]{0:T(128)}, f32[4]{0:T(128)S(1)}, u32[]{:S(2)}) copy-start(f32[4]{0:T(128)S(1)} %get-tuple-element.21642) | copy-start | bytes 52 | tf_op jit(solution)/shard_map/jvp()/while
  301.8 104.4 %copy-start.227 = (f32[4]{0:T(128)}, f32[4]{0:T(128)S(1)}, u32[]{:S(2)}) copy-start(f32[4]{0:T(128)S(1)} %get-tuple-element.21652) | copy-start | bytes 52 | tf_op jit(solution)/shard_map/jvp()/while
  301.9 104.4 %copy-start.229 = (f32[4]{0:T(128)}, f32[4]{0:T(128)S(1)}, u32[]{:S(2)}) copy-start(f32[4]{0:T(128)S(1)} %get-tuple-element.21662) | copy-start | bytes 52 | tf_op jit(solution)/shard_map/jvp()/while
  301.9 104.4 %copy-start.231 = (f32[4]{0:T(128)}, f32[4]{0:T(128)S(1)}, u32[]{:S(2)}) copy-start(f32[4]{0:T(128)S(1)} %get-tuple-element.21672) | copy-start | bytes 52 | tf_op jit(solution)/shard_map/jvp()/while
  302.0 104.3 %copy-start.233 = (f32[4]{0:T(128)}, f32[4]{0:T(128)S(1)}, u32[]{:S(2)}) copy-start(f32[4]{0:T(128)S(1)} %get-tuple-element.21682) | copy-start | bytes 52 | tf_op jit(solution)/shard_map/jvp()/while
  302.0 104.3 %copy-start.235 = (f32[4]{0:T(128)}, f32[4]{0:T(128)S(1)}, u32[]{:S(2)}) copy-start(f32[4]{0:T(128)S(1)} %get-tuple-element.21692) | copy-start | bytes 52 | tf_op jit(solution)/shard_map/jvp()/while
  302.1 104.2 %copy-start.196 = (f32[4]{0:T(128)}, f32[4]{0:T(128)S(1)}, u32[]{:S(2)}) copy-start(f32[4]{0:T(128)S(1)} %get-tuple-element.21712) | copy-start | bytes 52 | tf_op jit(solution)/shard_map/jvp()/while
  302.1 104.2 %copy-start.237 = (f32[4]{0:T(128)}, f32[4]{0:T(128)S(1)}, u32[]{:S(2)}) copy-start(f32[4]{0:T(128)S(1)} %get-tuple-element.21702) | copy-start | bytes 52 | tf_op jit(solution)/shard_map/jvp()/while
  482.7 108.4 %copy-start.100 = (f32[4,32,16]{2,1,0:T(8,128)S(1)}, f32[4,32,16]{2,1,0:T(8,128)}, u32[]{:S(2)}) copy-start(f32[4,32,16]{2,1,0:T(8,128)} %copy-done.99) | copy-start | bytes 24580 | tf_op jit(solution)/shard_map/jvp()/while
  482.7 108.3 %copy-start.192 = (f32[4,1,16]{2,1,0:T(1,128)S(1)}, f32[4,1,16]{2,1,0:T(1,128)}, u32[]{:S(2)}) copy-start(f32[4,1,16]{2,1,0:T(1,128)} %copy-done.191) | copy-start | bytes 772 | tf_op jit(solution)/shard_map/jvp()/while
  486.3 104.6 %copy-start.205 = (f32[4]{0:T(128)}, f32[4]{0:T(128)S(1)}, u32[]{:S(2)}) copy-start(f32[4]{0:T(128)S(1)} %get-tuple-element.21621) | copy-start | bytes 52 | tf_op jit(solution)/shard_map/jvp()/while
  486.3 104.6 %copy-start.221 = (f32[4]{0:T(128)}, f32[4]{0:T(128)S(1)}, u32[]{:S(2)}) copy-start(f32[4]{0:T(128)S(1)} %get-tuple-element.21632) | copy-start | bytes 52 | tf_op jit(solution)/shard_map/jvp()/while
  486.4 104.5 %copy-start.225 = (f32[4]{0:T(128)}, f32[4]{0:T(128)S(1)}, u32[]{:S(2)}) copy-start(f32[4]{0:T(128)S(1)} %get-tuple-element.21642) | copy-start | bytes 52 | tf_op jit(solution)/shard_map/jvp()/while
  486.4 104.5 %copy-start.227 = (f32[4]{0:T(128)}, f32[4]{0:T(128)S(1)}, u32[]{:S(2)}) copy-start(f32[4]{0:T(128)S(1)} %get-tuple-element.21652) | copy-start | bytes 52 | tf_op jit(solution)/shard_map/jvp()/while
  486.5 104.4 %copy-start.229 = (f32[4]{0:T(128)}, f32[4]{0:T(128)S(1)}, u32[]{:S(2)}) copy-start(f32[4]{0:T(128)S(1)} %get-tuple-element.21662) | copy-start | bytes 52 | tf_op jit(solution)/shard_map/jvp()/while
  486.5 104.4 %copy-start.231 = (f32[4]{0:T(128)}, f32[4]{0:T(128)S(1)}, u32[]{:S(2)}) copy-start(f32[4]{0:T(128)S(1)} %get-tuple-element.21672) | copy-start | bytes 52 | tf_op jit(solution)/shard_map/jvp()/while
  486.6 104.3 %copy-start.233 = (f32[4]{0:T(128)}, f32[4]{0:T(128)S(1)}, u32[]{:S(2)}) copy-start(f32[4]{0:T(128)S(1)} %get-tuple-element.21682) | copy-start | bytes 52 | tf_op jit(solution)/shard_map/jvp()/while
  486.6 104.3 %copy-start.235 = (f32[4]{0:T(128)}, f32[4]{0:T(128)S(1)}, u32[]{:S(2)}) copy-start(f32[4]{0:T(128)S(1)} %get-tuple-element.21692) | copy-start | bytes 52 | tf_op jit(solution)/shard_map/jvp()/while
  486.7 104.2 %copy-start.196 = (f32[4]{0:T(128)}, f32[4]{0:T(128)S(1)}, u32[]{:S(2)}) copy-start(f32[4]{0:T(128)S(1)} %get-tuple-element.21712) | copy-start | bytes 52 | tf_op jit(solution)/shard_map/jvp()/while
  486.7 104.2 %copy-start.237 = (f32[4]{0:T(128)}, f32[4]{0:T(128)S(1)}, u32[]{:S(2)}) copy-start(f32[4]{0:T(128)S(1)} %get-tuple-element.21702) | copy-start | bytes 52 | tf_op jit(solution)/shard_map/jvp()/while
  486.8 104.2 %copy-start.199 = (f32[4]{0:T(128)}, f32[4]{0:T(128)S(1)}, u32[]{:S(2)}) copy-start(f32[4]{0:T(128)S(1)} %get-tuple-element.21722) | copy-start | bytes 52 | tf_op jit(solution)/shard_map/jvp()/while
  667.5 108.3 %copy-start.100 = (f32[4,32,16]{2,1,0:T(8,128)S(1)}, f32[4,32,16]{2,1,0:T(8,128)}, u32[]{:S(2)}) copy-start(f32[4,32,16]{2,1,0:T(8,128)} %copy-done.99) | copy-start | bytes 24580 | tf_op jit(solution)/shard_map/jvp()/while
  667.5 108.3 %copy-start.192 = (f32[4,1,16]{2,1,0:T(1,128)S(1)}, f32[4,1,16]{2,1,0:T(1,128)}, u32[]{:S(2)}) copy-start(f32[4,1,16]{2,1,0:T(1,128)} %copy-done.191) | copy-start | bytes 772 | tf_op jit(solution)/shard_map/jvp()/while
  671.1 104.5 %copy-start.205 = (f32[4]{0:T(128)}, f32[4]{0:T(128)S(1)}, u32[]{:S(2)}) copy-start(f32[4]{0:T(128)S(1)} %get-tuple-element.21621) | copy-start | bytes 52 | tf_op jit(solution)/shard_map/jvp()/while
  671.1 104.5 %copy-start.221 = (f32[4]{0:T(128)}, f32[4]{0:T(128)S(1)}, u32[]{:S(2)}) copy-start(f32[4]{0:T(128)S(1)} %get-tuple-element.21632) | copy-start | bytes 52 | tf_op jit(solution)/shard_map/jvp()/while
  671.2 104.4 %copy-start.225 = (f32[4]{0:T(128)}, f32[4]{0:T(128)S(1)}, u32[]{:S(2)}) copy-start(f32[4]{0:T(128)S(1)} %get-tuple-element.21642) | copy-start | bytes 52 | tf_op jit(solution)/shard_map/jvp()/while
  671.2 104.4 %copy-start.227 = (f32[4]{0:T(128)}, f32[4]{0:T(128)S(1)}, u32[]{:S(2)}) copy-start(f32[4]{0:T(128)S(1)} %get-tuple-element.21652) | copy-start | bytes 52 | tf_op jit(solution)/shard_map/jvp()/while
  671.3 104.4 %copy-start.229 = (f32[4]{0:T(128)}, f32[4]{0:T(128)S(1)}, u32[]{:S(2)}) copy-start(f32[4]{0:T(128)S(1)} %get-tuple-element.21662) | copy-start | bytes 52 | tf_op jit(solution)/shard_map/jvp()/while
  671.3 104.4 %copy-start.231 = (f32[4]{0:T(128)}, f32[4]{0:T(128)S(1)}, u32[]{:S(2)}) copy-start(f32[4]{0:T(128)S(1)} %get-tuple-element.21672) | copy-start | bytes 52 | tf_op jit(solution)/shard_map/jvp()/while
  671.4 104.3 %copy-start.233 = (f32[4]{0:T(128)}, f32[4]{0:T(128)S(1)}, u32[]{:S(2)}) copy-start(f32[4]{0:T(128)S(1)} %get-tuple-element.21682) | copy-start | bytes 52 | tf_op jit(solution)/shard_map/jvp()/while
  671.4 104.3 %copy-start.235 = (f32[4]{0:T(128)}, f32[4]{0:T(128)S(1)}, u32[]{:S(2)}) copy-start(f32[4]{0:T(128)S(1)} %get-tuple-element.21692) | copy-start | bytes 52 | tf_op jit(solution)/shard_map/jvp()/while
  671.5 104.2 %copy-start.196 = (f32[4]{0:T(128)}, f32[4]{0:T(128)S(1)}, u32[]{:S(2)}) copy-start(f32[4]{0:T(128)S(1)} %get-tuple-element.21712) | copy-start | bytes 52 | tf_op jit(solution)/shard_map/jvp()/while
  671.5 104.2 %copy-start.237 = (f32[4]{0:T(128)}, f32[4]{0:T(128)S(1)}, u32[]{:S(2)}) copy-start(f32[4]{0:T(128)S(1)} %get-tuple-element.21702) | copy-start | bytes 52 | tf_op jit(solution)/shard_map/jvp()/while
  776.7 123.1 %all-gather.13.cloned.1.call-start = ((), (), s32[]{:S(2)}) async-start(), calls=%async_computation.10 | async-start | bytes 3244032 | tf_op jit(solution)/shard_map/all_gather | solution.py:18
  777.4 261.1 %all-gather.9.cloned.1.call-start = ((), (), s32[]{:S(2)}) async-start(), calls=%async_computation.6 | async-start | bytes 10616832 | tf_op jit(solution)/shard_map/all_gather | solution.py:198
  778.2 398.6 %all-gather.11.cloned.1.call-start = ((), (), s32[]{:S(2)}) async-start(), calls=%async_computation.7 | async-start | bytes 10616832 | tf_op jit(solution)/shard_map/all_gather | solution.py:199
  1006.4 249.8 %copy-start.150 = (f32[128]{0:T(128)}, f32[128]{0:T(128)S(1)}, u32[]{:S(2)}) copy-start(f32[128]{0:T(128)S(1)} %fusion.679) | copy-start | bytes 1540
  1008.6 12.1 all-to-all-start
  1046.9 168.6 %copy-start.2 = (f32[4,1,40,3072]{3,2,0,1:T(8,128)}, f32[4,1,40,3072]{3,2,0,1:T(8,128)S(1)}, u32[]{:S(2)}) copy-start(f32[4,1,40,3072]{3,2,0,1:T(8,128)S(1)} %fusion.586) | copy-start | bytes 5898244
  1186.1 12.7 all-to-all-start.1
  1243.0 12.1 all-to-all-start.3
  1246.6 103.6 %all-gather.17.cloned.1.call-start = ((), (), s32[]{:S(2)}) async-start(), calls=%async_computation.12 | async-start | bytes 3244032 | tf_op jit(solution)/shard_map/all_gather | solution.py:18
  1293.7 1421.4 %all-reduce.178.cloned.1.call-start = ((), (), s32[]{:S(2)}) async-start(), calls=%async_computation.13 | async-start | bytes 30081024 | tf_op jit(solution)/shard_map/psum | solution.py:286
  2157.3 3.1 collective-permute-start.1
  2170.6 715.3 %reduce-scatter.5.cloned.1.call-start = ((), (), s32[]{:S(2)}) async-start(), calls=%async_computation.9 | async-start | bytes 10616832 | tf_op jit(solution)/shard_map/reduce_scatter | solution.py:245
  2182.7 869.9 %reduce-scatter.3.cloned.1.call-start = ((), (), s32[]{:S(2)}) async-start(), calls=%async_computation.8 | async-start | bytes 10616832 | tf_op jit(solution)/shard_map/reduce_scatter | solution.py:244
  (564 other events, 14242.0 us)
Sparse Core Ops, SparseCore 0:
  776.8 61.6 all-gather.14
  842.0 57.7 all-gather.12
  902.0 136.5 all-gather.8
  1040.6 136.1 all-gather.10
  1293.8 56.3 all-gather.16
  2170.8 544.2 all-reduce.177
  2721.2 164.7 reduce-scatter.4
  2890.1 162.3 reduce-scatter.2
where the time goes:
time: 3120 us; the launch traced here: 3070 us
  local copies, waits for them, and re-layouts  1110 us (36%)
  waiting for transfers between devices  1100 us (35%)
  other arithmetic  544 us (17%)
  matrix products  135 us (4%)
  loops' own time  92.2 us (3%)
  blocking collectives  55.8 us (2%)
    psum x1, waiting for transfers between devices, per_device(): lax.psum((grad_mixer_gain, grad_in_proj, grad_conv_weight, grad_conv_bias...  460 us
    dynamic_update_slice x388, local copies, waits for them, and re-layouts, scan_part(): lax.scan(advance, jnp.zeros(decay_log.shape, jnp.float32), pieces)  453 us
    dynamic_slice x324, local copies, waits for them, and re-layouts, scan_part(): lax.scan(advance, jnp.zeros(decay_log.shape, jnp.float32), pieces)  285 us
    reduce_scatter x1, waiting for transfers between devices, per_device(): lax.psum_scatter(grad_down_full, 'seq', scatter_dimension=1, tiled=True)  171 us
    reduce_scatter x1, waiting for transfers between devices, per_device(): lax.psum_scatter(grad_up_full, 'seq', scatter_dimension=2, tiled=True)  167 us
    all_gather x3, waiting for transfers between devices, entering(): pieces = jax.tree.map(lambda part: lax.all_gather(part, axis), value)  137 us
    all_gather x1, waiting for transfers between devices, per_device(): lax.all_gather(expert_down, 'seq', axis=1, tiled=True)  130 us
    mul x196, other arithmetic, advance(): step_b[index] * act_b[index]  128 us
  transfers between devices with their start and end apart: 13, of which 12 were waited for; matrix products, arithmetic and copies ran while one was open for 6% of the time, Pallas kernels for 0%

commit v1 on v0

--- a/solution.py
+++ b/solution.py
@@ -1,3 +1,4 @@
+import functools
 import jax
 import jax.numpy as jnp
 from jax import lax
@@ -5,6 +6,41 @@
 
 precise = lax.Precision.HIGHEST
 epsilon = 1e-05
+
+
+def reach_tails(sheet, dim_i):
+    sheet = jnp.moveaxis(sheet, 0, dim_i)
+    front = sheet.shape
+    lower = sheet.reshape(*front[:dim_i], front[dim_i] * front[dim_i + 1], *front[dim_i + 2 :])
+    return lower
+
+
+def _create_case(q_in, across, array_dim):
+    ndev = lax.axis_size(across)
+    inbox = []
+    for u in range(ndev):
+        inbox.append((u, (u + 1) % ndev))
+    ledger = []
+    for ix, src_i in inbox:
+        ledger.append((src_i, ix))
+    current_value, newest = ([], [])
+    for s in range(ndev - 1):
+        if s % 2 == 0:
+            v_now = lax.ppermute(current_value[-1] if current_value else q_in, across, inbox)
+            current_value.append(v_now)
+        else:
+            moved = lax.ppermute(newest[-1] if newest else q_in, across, ledger)
+            newest.append(moved)
+    right_arr = jnp.stack([*current_value[::-1], q_in, *newest], axis=0)
+    met_up = lax.axis_index(across)
+    all_values = len(current_value)
+    z1 = met_up - all_values
+    right_arr = right_arr[(jnp.arange(ndev) - z1) % ndev]
+    outcome_arr = reach_tails(right_arr, array_dim)
+    return outcome_arr
+
+
+show_floor = functools.partial(_create_case, across="seq", array_dim=1)
 
 
 def passed_along(block, axis, distance):
@@ -196,7 +232,7 @@
     buffer = matmul_high(dispatch, normed_moe).reshape(experts_n, capacity, -1)
     full_up, full_down = (
         lax.all_gather(expert_up, "seq", axis=2, tiled=True),
-        lax.all_gather(expert_down, "seq", axis=1, tiled=True),
+        show_floor(expert_down),
     )
     received = lax.all_to_all(buffer, "exp", split_axis=0, concat_axis=0, tiled=True)
     local_n = full_up.shape[0]

time: 3120 us -> 3170 us (1.016)
    ppermute x0 -> x7, waiting for transfers between devices: none -> 180 us  [the longest x4 180 us: _create_case(): lax.ppermute(current_value[-1] if current_value else q_in, across, inbox)]
    all_gather x3, waiting for transfers between devices: 137 us -> 28.1 us  [entering(): pieces = jax.tree.map(lambda part: lax.all_gather(part, axis), value)]
    all_gather x1, waiting for transfers between devices: 130 us -> 92.7 us  [per_device(): lax.all_gather(expert_down, 'seq', axis=1, tiled=True)]
  transfers between devices with their start and end apart: 13 -> 21, of which waited for: 12 -> 12; matrix products, arithmetic and copies ran while one was open for 6% -> 8% of each run, Pallas kernels for 0% -> 0%
where the time goes in v1:
time: 3170 us; the launch traced here: 3120 us
  local copies, waits for them, and re-layouts  1130 us (36%)
  waiting for transfers between devices  1110 us (35%)
  other arithmetic  543 us (17%)
  matrix products  135 us (4%)
  loops' own time  95.1 us (3%)
  blocking collectives  44.7 us (1%)
  starting transfers between devices  38.4 us (1%)
    psum x1, waiting for transfers between devices, per_device(): lax.psum((grad_mixer_gain, grad_in_proj, grad_conv_weight, grad_conv_bias...  459 us
    dynamic_update_slice x388, local copies, waits for them, and re-layouts, scan_part(): lax.scan(advance, jnp.zeros(decay_log.shape, jnp.float32), pieces)  451 us
    dynamic_slice x324, local copies, waits for them, and re-layouts, scan_part(): lax.scan(advance, jnp.zeros(decay_log.shape, jnp.float32), pieces)  283 us
    ppermute x4, waiting for transfers between devices, _create_case(): lax.ppermute(current_value[-1] if current_value else q_in, across, inbox)  180 us
    reduce_scatter x1, waiting for transfers between devices, per_device(): lax.psum_scatter(grad_down_full, 'seq', scatter_dimension=1, tiled=True)  171 us
    reduce_scatter x1, waiting for transfers between devices, per_device(): lax.psum_scatter(grad_up_full, 'seq', scatter_dimension=2, tiled=True)  167 us
    mul x196, other arithmetic, advance(): step_b[index] * act_b[index]  128 us
    reduce_sum x8, other arithmetic, advance(): step_b[index][:, None] * decay_rate  111 us
  transfers between devices with their start and end apart: 21, of which 12 were waited for; matrix products, arithmetic and copies ran while one was open for 8% of the time, Pallas kernels for 0%

profile of v1, /device:TPU:0, one launch (start us, length us, event | category | flops | bytes accessed | tf_op | source)
XLA Modules:
  0.0 3120.2 jit_solution(6525605452506020187)
XLA Ops:
  9.0 7.8 fusion.628
  26.2 3.8 fusion.622
  31.8 3.1 fusion.707
  36.6 740.7 %while.750 = (s32[]{:T(128)}, f32[1536,16]{0,1:T(8,128)S(1)}, f32[4,32,1536]{2,1,0:T(8,128)}, f32[4,1536,1]{1,2,0:T(1,128)}, f32[4,1536,16]{1,2,0:T(8,128)}, /*i...) while((s32[]{:T(128)}, f32[1536,16]{0,1:T(8,128)S(1)}, ...), condition=%wide.region_36.37_spmd.clone, body=%wide.region_3.36_spmd.clone.sunk | while | flops 11132994 | bytes 24794744 | solution.py:171
  266.6 2.8 bitcast_dynamic-update-slice_fusion.115
  636.7 2.8 bitcast_dynamic-update-slice_fusion.115
  782.1 31.3 %collective-permute-done.1 = f32[1,384,768]{2,1,0:T(8,128)S(1)} collective-permute-done((f32[1,384,768]{2,1,0:T(8,128)}, f32[1,384,768]{2,1,0:T(8,128)S(1)}, u32[]{:S(2)}, u32[]{:S(2)}) %collective-permute-start.1) | collective-permute-done | bytes 1179680 | tf_op jit(solution)/shard_map/ppermute | solution.py:29
  814.4 4.7 collective-permute-start.5
  819.1 55.3 %collective-permute-done.2 = f32[1,384,768]{2,1,0:T(8,128)S(1)} collective-permute-done((f32[1,384,768]{2,1,0:T(8,128)S(1)}, f32[1,384,768]{2,1,0:T(8,128)S(1)}, u32[]{:S(2)}, u32[]{:S(2)}) %collective-permute-start.2) | collective-permute-done | bytes 1179680 | tf_op jit(solution)/shard_map/ppermute | solution.py:29
  880.4 50.7 %collective-permute-done.3 = f32[1,384,768]{2,1,0:T(8,128)} collective-permute-done((f32[1,384,768]{2,1,0:T(8,128)S(1)}, f32[1,384,768]{2,1,0:T(8,128)}, u32[]{:S(2)}, u32[]{:S(2)}) %collective-permute-start.3) | collective-permute-done | bytes 1179680 | tf_op jit(solution)/shard_map/ppermute | solution.py:29
  943.3 3.4 collective-permute-start.7
  946.6 43.0 %collective-permute-done.4 = f32[1,384,768]{2,1,0:T(8,128)} collective-permute-done((f32[1,384,768]{2,1,0:T(8,128)}, f32[1,384,768]{2,1,0:T(8,128)}, u32[]{:S(2)}, u32[]{:S(2)}) %collective-permute-start.4) | collective-permute-done | bytes 1179680 | tf_op jit(solution)/shard_map/ppermute | solution.py:29
  1000.1 5.3 copy.107
  1005.5 3.9 copy.120
  1009.3 68.6 %while.751 = (s32[]{:T(128)}, f32[1536,16]{0,1:T(8,128)S(1)}, s32[]{:T(128)}, f32[32,1536,16]{1,2,0:T(8,128)}, f32[32,1536,16]{1,0,2:T(8,128)}, /*index=5*/s32[]{:T(128)}, s32[]{:T(128)}) while((s32[]{:T(128)}, f32[1536,16]{0,1:T(8,128)S(1)}, s32[]{:T(128)}, f32[32,1536,16]{1,2,0:T(8,128)}, f32[32,1536,16]{1,0,2:T(8,128)}, ...), condition=%wide.region_40.41_spmd.clone, body=%wide.region_39.40_spmd.clone.sunk | while | flops 98308 | bytes 589929 | solution.py:66
  1078.9 25.3 while.749
  1083.6 6.1 multiply_dynamic-update-slice_fusion.38
  1096.2 6.3 multiply_dynamic-update-slice_fusion.38
  1106.3 5.6 multiply_reduce_fusion.141
  1114.0 3.6 all-to-all-start
  1122.4 8.6 gather_fusion
  1131.8 8.7 fusion.584
  1140.6 7.5 fusion.604
  1148.1 4.4 all-to-all-start.1
  1155.1 6.0 all-to-all-done.1
  1168.4 4.1 all-to-all-start.2
  1172.5 92.7 %all-gather.11.cloned.1.call-done = f32[1,3072,768]{2,1,0:T(8,128)} async-done(((f32[1,384,768]{2,1,0:T(8,128)}), f32[1,3072,768]{2,1,0:T(8,128)}) %all-gather.11.cloned.1.call-update) | async-done | bytes 9437200 | tf_op jit(solution)/shard_map/all_gather | solution.py:262
  1265.2 12.9 fusion.596
  1279.4 13.1 fusion.580
  1292.6 3.6 all-to-all-start.3
  1297.3 7.3 all-to-all-done.3
  1307.8 9.3 multiply_reduce_fusion.131
  1318.7 23.9 while.752
  1321.2 7.2 multiply_reduce_fusion.199
  1333.1 7.2 multiply_reduce_fusion.199
  1343.5 4.0 rev.6
  1349.0 15.4 reduce_window_sum.42
  1364.5 7.2 fusion.704
  1371.7 28.1 all-gather.17.cloned.1.call-done
  1399.8 5.4 copy.108
  1405.2 8.1 rev.7
  1413.3 68.2 %while.753 = (s32[]{:T(128)}, f32[1536,16]{0,1:T(8,128)S(1)}, s32[]{:T(128)}, f32[32,1536,16]{1,2,0:T(8,128)}, f32[32,1536,16]{1,0,2:T(8,128)}, /*index=5*/s32[]{:T(128)}, s32[]{:T(128)}) while((s32[]{:T(128)}, f32[1536,16]{0,1:T(8,128)S(1)}, s32[]{:T(128)}, f32[32,1536,16]{1,2,0:T(8,128)}, f32[32,1536,16]{1,0,2:T(8,128)}, ...), condition=%wide.region_60.61_spmd.clone, body=%wide.region_59.60_spmd.clone.sunk | while | flops 98308 | bytes 589929 | solution.py:66
  1484.8 708.3 %while.754 = (s32[]{:T(128)}, f32[1536,16]{0,1:T(8,128)}, f32[1536,16]{0,1:T(8,128)S(1)}, f32[4,32,1536]{2,1,0:T(8,128)}, f32[4,32,1536]{2,1,0:T(8,128)}, /*inde...) while((s32[]{:T(128)}, f32[1536,16]{0,1:T(8,128)}, ...), condition=%wide.region_190.191_spmd.clone, body=%wide.region_61.190_spmd.clone.sunk | while | flops 17356836 | bytes 57770112 | solution.py:171
  1513.4 12.8 multiply_reduce_fusion.200
  1555.6 15.0 multiply_reduce_fusion.201
  1659.0 2.8 multiply_add_fusion.56
  1690.2 12.8 multiply_reduce_fusion.200
  1732.4 15.0 multiply_reduce_fusion.201
  1835.9 2.8 multiply_add_fusion.56
  1867.1 12.8 multiply_reduce_fusion.200
  1909.4 15.0 multiply_reduce_fusion.201
  2013.0 2.8 multiply_add_fusion.56
  2044.2 12.8 multiply_reduce_fusion.200
  2086.4 15.0 multiply_reduce_fusion.201
  2190.0 2.8 multiply_add_fusion.56
  2207.7 10.1 fusion.602
  2219.4 11.4 convolution_bitcast_fusion
  2232.4 10.3 convolution_bitcast_fusion.1
  2244.3 12.1 multiply_reduce_fusion.137
  2256.5 44.7 %all-reduce.174 = (f32[768]{0:T(1024)}, f32[4,1536]{1,0:T(4,128)}, f32[1536]{0:T(1024)}, f32[1536]{0:T(1024)}, f32[1536]{0:T(1024)}, /*index=5*/f32[768]{0:T(102...) all-reduce(f32[768]{0:T(1024)S(1)} %get-tuple-element.12840, ...), channel_id=1, replica_groups=mesh['seq'=8,'exp'=4] {'seq','exp'}, use_global_device_ids=true, to_apply=%region_195.196 | all-reduce | flops 15368 | bytes 122944 | tf_op jit(solution)/shard_map/psum | solution.py:322
  2303.2 459.4 %all-reduce.178.cloned.1.call-done = (f32[768,3072]{1,0:T(8,128)}, f32[1536,80]{0,1:T(8,128)}, f32[48,1536]{1,0:T(8,128)}, f32[1536,16]{0,1:T(8,128)}, f32[1536,768]{1,0:T(8,128)}) async-done(((f32[768,3072]{1,0:T(8,128)}, f32[1536,80]{0,1:T(8,128)}, f32[48,1536]{1,0:T(8,128)}, f32[1536,16]{0,1:T(8,128)}, f32[1536,768]{1,0:T(8,128)}), (f32[768,3072]{1,0:T(8,128)}, f32[1536,80]{0,1:T(8,128)}, ...) | async-done | bytes 15040528 | tf_op jit(solution)/shard_map/psum | solution.py:322
  2762.6 170.9 %reduce-scatter.5.cloned.1.call-done = f32[1,384,768]{2,1,0:T(8,128)} async-done(((f32[1,3072,768]{2,1,0:T(8,128)}), f32[1,384,768]{2,1,0:T(8,128)}) %reduce-scatter.5.cloned.1.call-update) | async-done | bytes 1179664 | tf_op jit(solution)/shard_map/reduce_scatter | solution.py:281
  2933.4 166.6 %reduce-scatter.3.cloned.1.call-done = f32[1,768,384]{2,1,0:T(8,128)} async-done(((f32[1,768,3072]{2,1,0:T(8,128)}), f32[1,768,384]{2,1,0:T(8,128)}) %reduce-scatter.3.cloned.1.call-update) | async-done | bytes 1179664 | tf_op jit(solution)/shard_map/reduce_scatter | solution.py:280
  3100.0 8.8 copy.1519
  (3632 shorter events, 1489.1 us)
Async XLA Ops:
  7.2 992.9 %all-gather.15.cloned.1.call-start = ((), (), s32[]{:S(2)}) async-start(), calls=%async_computation.11 | async-start | bytes 3244032 | tf_op jit(solution)/shard_map/all_gather | solution.py:54
  16.8 9.4 collective-permute-start
  113.8 107.9 %copy-start.104 = (f32[4,32,16]{2,1,0:T(8,128)S(1)}, f32[4,32,16]{2,1,0:T(8,128)}, u32[]{:S(2)}) copy-start(f32[4,32,16]{2,1,0:T(8,128)} %copy-done.103) | copy-start | bytes 24580 | tf_op jit(solution)/shard_map/jvp()/while
  113.8 107.9 %copy-start.194 = (f32[4,1,16]{2,1,0:T(1,128)S(1)}, f32[4,1,16]{2,1,0:T(1,128)}, u32[]{:S(2)}) copy-start(f32[4,1,16]{2,1,0:T(1,128)} %copy-done.193) | copy-start | bytes 772 | tf_op jit(solution)/shard_map/jvp()/while
  117.4 104.2 %copy-start.216 = (f32[4]{0:T(128)}, f32[4]{0:T(128)S(1)}, u32[]{:S(2)}) copy-start(f32[4]{0:T(128)S(1)} %get-tuple-element.21621) | copy-start | bytes 52 | tf_op jit(solution)/shard_map/jvp()/while
  117.4 104.2 %copy-start.223 = (f32[4]{0:T(128)}, f32[4]{0:T(128)S(1)}, u32[]{:S(2)}) copy-start(f32[4]{0:T(128)S(1)} %get-tuple-element.21632) | copy-start | bytes 52 | tf_op jit(solution)/shard_map/jvp()/while
  117.5 104.1 %copy-start.227 = (f32[4]{0:T(128)}, f32[4]{0:T(128)S(1)}, u32[]{:S(2)}) copy-start(f32[4]{0:T(128)S(1)} %get-tuple-element.21642) | copy-start | bytes 52 | tf_op jit(solution)/shard_map/jvp()/while
  117.5 104.1 %copy-start.229 = (f32[4]{0:T(128)}, f32[4]{0:T(128)S(1)}, u32[]{:S(2)}) copy-start(f32[4]{0:T(128)S(1)} %get-tuple-element.21652) | copy-start | bytes 52 | tf_op jit(solution)/shard_map/jvp()/while
  117.6 104.0 %copy-start.231 = (f32[4]{0:T(128)}, f32[4]{0:T(128)S(1)}, u32[]{:S(2)}) copy-start(f32[4]{0:T(128)S(1)} %get-tuple-element.21662) | copy-start | bytes 52 | tf_op jit(solution)/shard_map/jvp()/while
  117.6 104.0 %copy-start.233 = (f32[4]{0:T(128)}, f32[4]{0:T(128)S(1)}, u32[]{:S(2)}) copy-start(f32[4]{0:T(128)S(1)} %get-tuple-element.21672) | copy-start | bytes 52 | tf_op jit(solution)/shard_map/jvp()/while
  117.7 103.9 %copy-start.235 = (f32[4]{0:T(128)}, f32[4]{0:T(128)S(1)}, u32[]{:S(2)}) copy-start(f32[4]{0:T(128)S(1)} %get-tuple-element.21682) | copy-start | bytes 52 | tf_op jit(solution)/shard_map/jvp()/while
  117.7 103.9 %copy-start.237 = (f32[4]{0:T(128)}, f32[4]{0:T(128)S(1)}, u32[]{:S(2)}) copy-start(f32[4]{0:T(128)S(1)} %get-tuple-element.21692) | copy-start | bytes 52 | tf_op jit(solution)/shard_map/jvp()/while
  298.9 107.9 %copy-start.104 = (f32[4,32,16]{2,1,0:T(8,128)S(1)}, f32[4,32,16]{2,1,0:T(8,128)}, u32[]{:S(2)}) copy-start(f32[4,32,16]{2,1,0:T(8,128)} %copy-done.103) | copy-start | bytes 24580 | tf_op jit(solution)/shard_map/jvp()/while
  298.9 107.9 %copy-start.194 = (f32[4,1,16]{2,1,0:T(1,128)S(1)}, f32[4,1,16]{2,1,0:T(1,128)}, u32[]{:S(2)}) copy-start(f32[4,1,16]{2,1,0:T(1,128)} %copy-done.193) | copy-start | bytes 772 | tf_op jit(solution)/shard_map/jvp()/while
  302.5 104.1 %copy-start.216 = (f32[4]{0:T(128)}, f32[4]{0:T(128)S(1)}, u32[]{:S(2)}) copy-start(f32[4]{0:T(128)S(1)} %get-tuple-element.21621) | copy-start | bytes 52 | tf_op jit(solution)/shard_map/jvp()/while
  302.6 104.1 %copy-start.223 = (f32[4]{0:T(128)}, f32[4]{0:T(128)S(1)}, u32[]{:S(2)}) copy-start(f32[4]{0:T(128)S(1)} %get-tuple-element.21632) | copy-start | bytes 52 | tf_op jit(solution)/shard_map/jvp()/while
  302.6 104.0 %copy-start.227 = (f32[4]{0:T(128)}, f32[4]{0:T(128)S(1)}, u32[]{:S(2)}) copy-start(f32[4]{0:T(128)S(1)} %get-tuple-element.21642) | copy-start | bytes 52 | tf_op jit(solution)/shard_map/jvp()/while
  302.7 104.0 %copy-start.229 = (f32[4]{0:T(128)}, f32[4]{0:T(128)S(1)}, u32[]{:S(2)}) copy-start(f32[4]{0:T(128)S(1)} %get-tuple-element.21652) | copy-start | bytes 52 | tf_op jit(solution)/shard_map/jvp()/while
  302.7 104.0 %copy-start.231 = (f32[4]{0:T(128)}, f32[4]{0:T(128)S(1)}, u32[]{:S(2)}) copy-start(f32[4]{0:T(128)S(1)} %get-tuple-element.21662) | copy-start | bytes 52 | tf_op jit(solution)/shard_map/jvp()/while
  302.8 104.0 %copy-start.233 = (f32[4]{0:T(128)}, f32[4]{0:T(128)S(1)}, u32[]{:S(2)}) copy-start(f32[4]{0:T(128)S(1)} %get-tuple-element.21672) | copy-start | bytes 52 | tf_op jit(solution)/shard_map/jvp()/while
  302.8 103.9 %copy-start.235 = (f32[4]{0:T(128)}, f32[4]{0:T(128)S(1)}, u32[]{:S(2)}) copy-start(f32[4]{0:T(128)S(1)} %get-tuple-element.21682) | copy-start | bytes 52 | tf_op jit(solution)/shard_map/jvp()/while
  483.9 108.0 %copy-start.104 = (f32[4,32,16]{2,1,0:T(8,128)S(1)}, f32[4,32,16]{2,1,0:T(8,128)}, u32[]{:S(2)}) copy-start(f32[4,32,16]{2,1,0:T(8,128)} %copy-done.103) | copy-start | bytes 24580 | tf_op jit(solution)/shard_map/jvp()/while
  483.9 108.0 %copy-start.194 = (f32[4,1,16]{2,1,0:T(1,128)S(1)}, f32[4,1,16]{2,1,0:T(1,128)}, u32[]{:S(2)}) copy-start(f32[4,1,16]{2,1,0:T(1,128)} %copy-done.193) | copy-start | bytes 772 | tf_op jit(solution)/shard_map/jvp()/while
  487.5 104.2 %copy-start.216 = (f32[4]{0:T(128)}, f32[4]{0:T(128)S(1)}, u32[]{:S(2)}) copy-start(f32[4]{0:T(128)S(1)} %get-tuple-element.21621) | copy-start | bytes 52 | tf_op jit(solution)/shard_map/jvp()/while
  487.5 104.2 %copy-start.223 = (f32[4]{0:T(128)}, f32[4]{0:T(128)S(1)}, u32[]{:S(2)}) copy-start(f32[4]{0:T(128)S(1)} %get-tuple-element.21632) | copy-start | bytes 52 | tf_op jit(solution)/shard_map/jvp()/while
  487.6 104.1 %copy-start.227 = (f32[4]{0:T(128)}, f32[4]{0:T(128)S(1)}, u32[]{:S(2)}) copy-start(f32[4]{0:T(128)S(1)} %get-tuple-element.21642) | copy-start | bytes 52 | tf_op jit(solution)/shard_map/jvp()/while
  487.6 104.1 %copy-start.229 = (f32[4]{0:T(128)}, f32[4]{0:T(128)S(1)}, u32[]{:S(2)}) copy-start(f32[4]{0:T(128)S(1)} %get-tuple-element.21652) | copy-start | bytes 52 | tf_op jit(solution)/shard_map/jvp()/while
  487.7 104.0 %copy-start.231 = (f32[4]{0:T(128)}, f32[4]{0:T(128)S(1)}, u32[]{:S(2)}) copy-start(f32[4]{0:T(128)S(1)} %get-tuple-element.21662) | copy-start | bytes 52 | tf_op jit(solution)/shard_map/jvp()/while
  487.7 104.0 %copy-start.233 = (f32[4]{0:T(128)}, f32[4]{0:T(128)S(1)}, u32[]{:S(2)}) copy-start(f32[4]{0:T(128)S(1)} %get-tuple-element.21672) | copy-start | bytes 52 | tf_op jit(solution)/shard_map/jvp()/while
  487.8 103.9 %copy-start.235 = (f32[4]{0:T(128)}, f32[4]{0:T(128)S(1)}, u32[]{:S(2)}) copy-start(f32[4]{0:T(128)S(1)} %get-tuple-element.21682) | copy-start | bytes 52 | tf_op jit(solution)/shard_map/jvp()/while
  487.8 103.9 %copy-start.237 = (f32[4]{0:T(128)}, f32[4]{0:T(128)S(1)}, u32[]{:S(2)}) copy-start(f32[4]{0:T(128)S(1)} %get-tuple-element.21692) | copy-start | bytes 52 | tf_op jit(solution)/shard_map/jvp()/while
  668.9 108.0 %copy-start.104 = (f32[4,32,16]{2,1,0:T(8,128)S(1)}, f32[4,32,16]{2,1,0:T(8,128)}, u32[]{:S(2)}) copy-start(f32[4,32,16]{2,1,0:T(8,128)} %copy-done.103) | copy-start | bytes 24580 | tf_op jit(solution)/shard_map/jvp()/while
  668.9 108.0 %copy-start.194 = (f32[4,1,16]{2,1,0:T(1,128)S(1)}, f32[4,1,16]{2,1,0:T(1,128)}, u32[]{:S(2)}) copy-start(f32[4,1,16]{2,1,0:T(1,128)} %copy-done.193) | copy-start | bytes 772 | tf_op jit(solution)/shard_map/jvp()/while
  672.6 104.2 %copy-start.216 = (f32[4]{0:T(128)}, f32[4]{0:T(128)S(1)}, u32[]{:S(2)}) copy-start(f32[4]{0:T(128)S(1)} %get-tuple-element.21621) | copy-start | bytes 52 | tf_op jit(solution)/shard_map/jvp()/while
  672.6 104.2 %copy-start.223 = (f32[4]{0:T(128)}, f32[4]{0:T(128)S(1)}, u32[]{:S(2)}) copy-start(f32[4]{0:T(128)S(1)} %get-tuple-element.21632) | copy-start | bytes 52 | tf_op jit(solution)/shard_map/jvp()/while
  672.7 104.1 %copy-start.227 = (f32[4]{0:T(128)}, f32[4]{0:T(128)S(1)}, u32[]{:S(2)}) copy-start(f32[4]{0:T(128)S(1)} %get-tuple-element.21642) | copy-start | bytes 52 | tf_op jit(solution)/shard_map/jvp()/while
  672.7 104.1 %copy-start.229 = (f32[4]{0:T(128)}, f32[4]{0:T(128)S(1)}, u32[]{:S(2)}) copy-start(f32[4]{0:T(128)S(1)} %get-tuple-element.21652) | copy-start | bytes 52 | tf_op jit(solution)/shard_map/jvp()/while
  672.8 104.0 %copy-start.231 = (f32[4]{0:T(128)}, f32[4]{0:T(128)S(1)}, u32[]{:S(2)}) copy-start(f32[4]{0:T(128)S(1)} %get-tuple-element.21662) | copy-start | bytes 52 | tf_op jit(solution)/shard_map/jvp()/while
  672.8 104.0 %copy-start.233 = (f32[4]{0:T(128)}, f32[4]{0:T(128)S(1)}, u32[]{:S(2)}) copy-start(f32[4]{0:T(128)S(1)} %get-tuple-element.21672) | copy-start | bytes 52 | tf_op jit(solution)/shard_map/jvp()/while
  672.9 103.9 %copy-start.235 = (f32[4]{0:T(128)}, f32[4]{0:T(128)S(1)}, u32[]{:S(2)}) copy-start(f32[4]{0:T(128)S(1)} %get-tuple-element.21682) | copy-start | bytes 52 | tf_op jit(solution)/shard_map/jvp()/while
  672.9 103.9 %copy-start.237 = (f32[4]{0:T(128)}, f32[4]{0:T(128)S(1)}, u32[]{:S(2)}) copy-start(f32[4]{0:T(128)S(1)} %get-tuple-element.21692) | copy-start | bytes 52 | tf_op jit(solution)/shard_map/jvp()/while
  778.0 227.5 %all-gather.13.cloned.1.call-start = ((), (), s32[]{:S(2)}) async-start(), calls=%async_computation.10 | async-start | bytes 3244032 | tf_op jit(solution)/shard_map/all_gather | solution.py:54
  778.7 353.1 %all-gather.9.cloned.1.call-start = ((), (), s32[]{:S(2)}) async-start(), calls=%async_computation.6 | async-start | bytes 10616832 | tf_op jit(solution)/shard_map/all_gather | solution.py:234
  779.5 485.7 %all-gather.11.cloned.1.call-start = ((), (), s32[]{:S(2)}) async-start(), calls=%async_computation.7 | async-start | bytes 10616832 | tf_op jit(solution)/shard_map/all_gather | solution.py:262
  779.5 33.8 %collective-permute-start.1 = (f32[1,384,768]{2,1,0:T(8,128)}, f32[1,384,768]{2,1,0:T(8,128)S(1)}, u32[]{:S(2)}, u32[]{:S(2)}) collective-permute-start(f32[1,384,768]{2,1,0:T(8,128)} %param.47), channel_id=1, source_target_pairs={{0,4},{4,8},{8,12},{12,16},{16,20},{20,24},{24,28},{28,0},{1,5},{5... | collective-permute-start | bytes 3538952 | tf_op jit(solution)/shard_map/ppermute | solution.py:29
  814.3 60.0 %collective-permute-start.2 = (f32[1,384,768]{2,1,0:T(8,128)S(1)}, f32[1,384,768]{2,1,0:T(8,128)S(1)}, u32[]{:S(2)}, u32[]{:S(2)}) collective-permute-start(f32[1,384,768]{2,1,0:T(8,128)S(1)} %collective-permute-done.1), channel_id=1, source_target_pairs={{0,4},{4,8},{8,12},{12,16},{16,20},{20,24},{24,28},{28,0},{1,5},{5... | collective-permute-start | bytes 3538952 | tf_op jit(solution)/shard_map/ppermute | solution.py:29
  814.4 63.8 %collective-permute-start.5 = (f32[1,384,768]{2,1,0:T(8,128)}, f32[1,384,768]{2,1,0:T(8,128)}, u32[]{:S(2)}, u32[]{:S(2)}) collective-permute-start(f32[1,384,768]{2,1,0:T(8,128)} %param.47), channel_id=1, source_target_pairs={{4,0},{8,4},{12,8},{16,12},{20,16},{24,20},{28,24},{0,28},{5,1},{9... | collective-permute-start | bytes 3538952 | tf_op jit(solution)/shard_map/ppermute | solution.py:32
  874.4 56.8 %collective-permute-start.3 = (f32[1,384,768]{2,1,0:T(8,128)S(1)}, f32[1,384,768]{2,1,0:T(8,128)}, u32[]{:S(2)}, u32[]{:S(2)}) collective-permute-start(f32[1,384,768]{2,1,0:T(8,128)S(1)} %collective-permute-done.2), channel_id=1, source_target_pairs={{0,4},{4,8},{8,12},{12,16},{16,20},{20,24},{24,28},{28,0},{1,5},{5... | collective-permute-start | bytes 3538952 | tf_op jit(solution)/shard_map/ppermute | solution.py:29
  878.2 65.1 %collective-permute-start.6 = (f32[1,384,768]{2,1,0:T(8,128)}, f32[1,384,768]{2,1,0:T(8,128)}, u32[]{:S(2)}, u32[]{:S(2)}) collective-permute-start(f32[1,384,768]{2,1,0:T(8,128)} %collective-permute-done.5), channel_id=1, source_target_pairs={{4,0},{8,4},{12,8},{16,12},{20,16},{24,20},{28,24},{0,28},{5,1},{9... | collective-permute-start | bytes 3538952 | tf_op jit(solution)/shard_map/ppermute | solution.py:32
  931.1 58.5 %collective-permute-start.4 = (f32[1,384,768]{2,1,0:T(8,128)}, f32[1,384,768]{2,1,0:T(8,128)}, u32[]{:S(2)}, u32[]{:S(2)}) collective-permute-start(f32[1,384,768]{2,1,0:T(8,128)} %collective-permute-done.3), channel_id=1, source_target_pairs={{0,4},{4,8},{8,12},{12,16},{16,20},{20,24},{24,28},{28,0},{1,5},{5... | collective-permute-start | bytes 3538952 | tf_op jit(solution)/shard_map/ppermute | solution.py:29
  943.3 176.8 %collective-permute-start.7 = (f32[1,384,768]{2,1,0:T(8,128)}, f32[1,384,768]{2,1,0:T(8,128)}, u32[]{:S(2)}, u32[]{:S(2)}) collective-permute-start(f32[1,384,768]{2,1,0:T(8,128)} %collective-permute-done.6), channel_id=1, source_target_pairs={{4,0},{8,4},{12,8},{16,12},{20,16},{24,20},{28,24},{0,28},{5,1},{9... | collective-permute-start | bytes 3538952 | tf_op jit(solution)/shard_map/ppermute | solution.py:32
  1111.9 194.0 %copy-start.154 = (f32[128]{0:T(128)}, f32[128]{0:T(128)S(1)}, u32[]{:S(2)}) copy-start(f32[128]{0:T(128)S(1)} %fusion.683) | copy-start | bytes 1540
  1114.0 17.0 all-to-all-start
  1140.5 124.6 %copy-start.3 = (f32[4,1,40,3072]{3,2,0,1:T(8,128)}, f32[4,1,40,3072]{3,2,0,1:T(8,128)S(1)}, u32[]{:S(2)}) copy-start(f32[4,1,40,3072]{3,2,0,1:T(8,128)S(1)} %fusion.584) | copy-start | bytes 5898244
  1148.1 12.9 all-to-all-start.1
  1154.0 142.7 %copy-start.134 = (f32[128,4]{0,1:T(4,128)}, f32[128,4]{0,1:T(4,128)S(1)}, u32[]{:S(2)}) copy-start(f32[128,4]{0,1:T(4,128)S(1)} %get-tuple-element.14993) | copy-start | bytes 6148
  1154.0 142.7 %copy-start.156 = (f32[128]{0:T(128)}, f32[128]{0:T(128)S(1)}, u32[]{:S(2)}) copy-start(f32[128]{0:T(128)S(1)} %get-tuple-element.14992) | copy-start | bytes 1540
  1168.4 96.8 %all-to-all-start.2 = ((f32[4,40,768]{2,1,0:T(8,128)}), f32[4,40,768]{2,1,0:T(8,128)}, u32[]{:S(2)}, u32[]{:S(2)}) async-start(f32[4,40,768]{2,1,0:T(8,128)} %bitcast.2493), calls=%async_computation.2 | async-start | bytes 983040 | tf_op jit(solution)/shard_map/all_to_all | solution.py:259
  1292.6 12.1 all-to-all-start.3
  1296.2 103.6 %all-gather.17.cloned.1.call-start = ((), (), s32[]{:S(2)}) async-start(), calls=%async_computation.12 | async-start | bytes 3244032 | tf_op jit(solution)/shard_map/all_gather | solution.py:54
  1343.3 1419.3 %all-reduce.178.cloned.1.call-start = ((), (), s32[]{:S(2)}) async-start(), calls=%async_computation.13 | async-start | bytes 30081024 | tf_op jit(solution)/shard_map/psum | solution.py:322
  2204.5 3.1 collective-permute-start.8
  2217.8 715.6 %reduce-scatter.5.cloned.1.call-start = ((), (), s32[]{:S(2)}) async-start(), calls=%async_computation.9 | async-start | bytes 10616832 | tf_op jit(solution)/shard_map/reduce_scatter | solution.py:281
  2230.8 869.2 %reduce-scatter.3.cloned.1.call-start = ((), (), s32[]{:S(2)}) async-start(), calls=%async_computation.8 | async-start | bytes 10616832 | tf_op jit(solution)/shard_map/reduce_scatter | solution.py:280
  (574 other events, 15185.8 us)
Sparse Core Ops, SparseCore 0:
  778.1 105.7 all-gather.14
  887.4 91.5 all-gather.12
  981.1 145.8 all-gather.8
  1129.0 136.1 all-gather.10
  1343.4 56.3 all-gather.16
  2218.0 544.5 all-reduce.177
  2768.6 164.7 reduce-scatter.4
  2937.6 162.3 reduce-scatter.2
